TPU v7x, 512 devices: a whole 4x8x8 slice. The times are simulated.
512 devices in a mesh: chan: 32 (over z, y_hi), seg: 16 (over x, y_lo, core).
Axes of the slice: x: 4, y: 8 (y_hi: 4, y_lo: 2; y = y_hi * 2 + y_lo), z: 8, core: 2. Of those that a mesh axis runs over, the one named last changes fastest.
Arguments:
- strain: float32 [1024, 40000], P('chan', 'seg')
- source_channels: int32 [32], replicated, may hold values from 0 to 1023, as said below
Outputs:
- stack: float32 [32, 1024, 501], P('seg', 'chan')
Inputs may be any that keep to these rules, and one draw needn't show every extreme that they name: `source_channels`: distinct channels; channel 0 and channel 1024 - 1 are always among them.
All inputs are finite; a program needn't handle non-finite values.
Results may differ from a plain program's by a relative error of at most 0.0001.
Values sent between devices are 32-bit elements; how exact they have to be, the bound alone decides.
A program may use at most 64 MiB of HBM per device.

v0:
```python
import math

import jax
import jax.numpy as jnp
from jax import lax
from jax.sharding import PartitionSpec as P

SEG_LEN = 625
TAPS = 63
MAXLAG = 250


cutoff = 0.1
water_level = 0.5
epsilon = 1e-06
block_width = 128


def from_behind(value, axis, steps):
    count = lax.axis_size(axis)
    leading, last = (max(0, -steps), min(count, count - steps))
    return lax.ppermute(value, axis, [(source, source + steps) for source in range(leading, last)])


def tap_shape(position, count):
    window = 0.54 - 0.46 * jnp.cos(2.0 * math.pi * position / (count - 1))
    return window * 2.0 * cutoff * jnp.sinc(2.0 * cutoff * (position - (count - 1) / 2.0))


def band_table(count):
    total = jnp.sum(tap_shape(jnp.arange(count).astype(jnp.float32), count))
    span = 5 * block_width
    offsets = jnp.arange(span)[:, None] - 4 * jnp.arange(block_width)[None, :]
    valid = (offsets >= 0) & (offsets <= count - 1)
    values = tap_shape((count - 1 - offsets).astype(jnp.float32), count) / total
    return jnp.where(valid, values, 0.0)


def decimate(extended, seg_len):
    channel_count = extended.shape[0]
    blocks = -(-seg_len // block_width)
    span = 5 * block_width
    stride = 4 * block_width
    needed = stride * (blocks - 1) + span
    extended = jnp.pad(extended, ((0, 0), (0, needed - extended.shape[1])))
    windows = jnp.stack(
        [
            extended[:, stride * block_index : stride * block_index + span]
            for block_index in range(blocks)
        ],
        axis=1,
    )
    outputs = jnp.einsum("rbi,im->rbm", windows, band_table(TAPS), precision=lax.Precision.HIGHEST)
    return outputs.reshape(channel_count, blocks * block_width)[:, :seg_len]


def forward_table(seg_len, block_index):
    samples = jnp.arange(seg_len)[:, None]
    freqs = block_index * block_width + jnp.arange(block_width)[None, :]
    phase = jnp.mod(samples * freqs, 2 * seg_len).astype(jnp.float32) * (math.pi / seg_len)
    valid = freqs <= seg_len
    return jnp.concatenate(
        [jnp.where(valid, jnp.cos(phase), 0.0), jnp.where(valid, -jnp.sin(phase), 0.0)], axis=1
    )


def inverse_table(block_index, factor):
    freqs = block_index * block_width + jnp.arange(block_width)[:, None]
    lag_values = jnp.arange(2 * MAXLAG + 1)[None, :] - MAXLAG
    phase = jnp.mod(freqs * lag_values, 2 * SEG_LEN).astype(jnp.float32) * (math.pi / SEG_LEN)
    weight = jnp.where((freqs == 0) | (freqs == SEG_LEN), 1.0, 2.0) * factor
    weight = jnp.where(freqs <= SEG_LEN, weight, 0.0)
    return jnp.concatenate([weight * jnp.cos(phase), -weight * jnp.sin(phase)], axis=0)


def whiten(real_part, imag_part, seg_len):
    power = real_part * real_part + imag_part * imag_part
    bin_span = power.shape[1]
    padded = jnp.pad(power, ((0, 0), (2, 2)))
    smooth = (
        padded[:, 0:bin_span]
        + padded[:, 1 : bin_span + 1]
        + padded[:, 2 : bin_span + 2]
        + padded[:, 3 : bin_span + 3]
        + padded[:, 4 : bin_span + 4]
    ) / 5.0
    floor_level = water_level * (jnp.sum(power, axis=1, keepdims=True) / (seg_len + 1))
    inverse_norm = 1.0 / jnp.sqrt(jnp.maximum(smooth, floor_level) + epsilon)
    return (real_part * inverse_norm, imag_part * inverse_norm)


def whitened_spectra(traces):
    seg_len = traces.shape[1]
    blocks = (seg_len + block_width) // block_width
    real_parts = []
    imag_parts = []
    for block_index in range(blocks):
        product = jnp.dot(
            traces,
            forward_table(seg_len, block_index),
            precision=lax.Precision.HIGHEST,
            preferred_element_type=jnp.float32,
        )
        real_parts.append(product[:, :block_width])
        imag_parts.append(product[:, block_width:])
    real_part, imag_part = whiten(
        jnp.concatenate(real_parts, 1), jnp.concatenate(imag_parts, 1), seg_len
    )
    return jnp.stack([real_part, imag_part], axis=1)


def back_block(cross_re, cross_im, block_index, factor):
    joined = jnp.concatenate([cross_re, cross_im], axis=2)
    return jnp.einsum(
        "sck,kl->scl", joined, inverse_table(block_index, factor), precision=lax.Precision.HIGHEST
    )


def correlate(sources, channels, factor):
    blocks = sources.shape[2] // block_width
    total = jnp.zeros((sources.shape[0], channels.shape[0], 2 * MAXLAG + 1), jnp.float32)
    for block_index in range(blocks):
        first_bin = block_index * block_width
        src_re = sources[:, 0, first_bin : first_bin + block_width]
        src_im = sources[:, 1, first_bin : first_bin + block_width]
        chan_re = channels[:, 0, first_bin : first_bin + block_width]
        chan_im = channels[:, 1, first_bin : first_bin + block_width]
        cross_re = (
            src_re[:, None, :] * chan_re[None, :, :] + src_im[:, None, :] * chan_im[None, :, :]
        )
        cross_im = (
            src_re[:, None, :] * chan_im[None, :, :] - src_im[:, None, :] * chan_re[None, :, :]
        )
        total = total + back_block(cross_re, cross_im, block_index, factor)
    return total


def collect_sources(chan_spec, picked_index, inside):
    picked = jnp.where(inside[:, None, None], jnp.take(chan_spec, picked_index, axis=0), 0.0)
    return lax.psum(picked, "chan")


def body(strain, source_channels):
    channel_count = strain.shape[0]
    margin = TAPS - 3
    last_samples = strain[:, strain.shape[1] - margin :]
    before = from_behind(last_samples, "seg", 1)
    extended = jnp.concatenate([before, strain], axis=1)
    traces = decimate(extended, SEG_LEN)
    segments = lax.axis_size("seg")
    factor = 1.0 / math.sqrt(2.0 * SEG_LEN * segments)
    base = lax.axis_index("chan") * channel_count
    local = source_channels - base
    inside = (local >= 0) & (local < channel_count)
    picked_index = jnp.clip(local, 0, channel_count - 1)
    chan_spec = whitened_spectra(traces)
    collected = collect_sources(chan_spec, picked_index, inside)
    return lax.psum_scatter(
        correlate(collected, chan_spec, factor), "seg", scatter_dimension=0, tiled=True
    )


def solution(mesh):
    in_specs = (P("chan", "seg"), P())
    out_specs = P("seg", "chan", None)
    return jax.shard_map(body, mesh=mesh, in_specs=in_specs, out_specs=out_specs, check_vma=False)
```

profile of v0, /device:TPU:1, one launch (start us, length us, event | category | flops | bytes accessed | tf_op | source)
XLA Modules:
  0.0 419.8 jit_solution(7290643064510937001)
XLA Ops:
  6.5 0.0 all-reduce.4.cloned.1.call-start
  6.5 0.8 slice.131
  7.3 4.6 %collective-permute-start = (f32[32,60]{1,0:T(8,128)S(1)}, f32[32,60]{1,0:T(8,128)S(1)}, u32[]{:S(2)}, u32[]{:S(2)}) collective-permute-start(f32[32,60]{1,0:T(8,128)S(1)} %slice.131), channel_id=1, source_target_pairs={{0,1},{1,2},{2,3},{3,4},{4,5},{5,6},{6,7},{7,8},{8,9},{9,10},{10,1... | collective-permute-start | bytes 23048 | tf_op jit(solution)/shard_map/ppermute | solution.py:22
  12.1 0.7 compare_and_fusion
  12.8 1.4 cosine_select_fusion.4
  14.1 1.4 cosine_select_fusion
  15.5 1.4 cosine_select_fusion.1
  16.9 0.0 copy-start
  16.9 1.4 cosine_select_fusion.2
  18.2 1.4 cosine_select_fusion.3
  19.6 5.5 %cosine_multiply_fusion = (f32[128,501]{0,1:T(8,128)S(1)}, f32[128,501]{0,1:T(8,128)S(1)}, f32[128,501]{0,1:T(8,128)S(1)}, f32[128,501]{0,1:T(8,128)S(1)}, f32[1...) fusion(s32[128]{0:T(128)S(1)} %iota_add_fusion.1, ...), kind=kLoop, calls=%fused_computation.165 | loop fusion | flops 3527040 | bytes 2574292 | tf_op jit(solution)/shard_map/mul | solution.py:73
  25.1 0.7 fusion.176
  25.7 0.0 collective-permute-done
  25.7 0.0 copy-done
  25.8 0.1 fusion.153
  25.8 0.1 bitcast_dynamic-update-slice_fusion.2
  25.9 0.1 bitcast_dynamic-update-slice_fusion.1
  26.0 0.1 bitcast_dynamic-update-slice_fusion
  26.1 0.1 pad_maximum_fusion
  26.3 2.8 convolution_bitcast_fusion
  29.1 0.4 fusion.19
  29.5 0.4 fusion.35
  29.9 0.4 fusion.31
  30.4 0.4 fusion.27
  30.8 0.4 fusion.23
  31.3 0.1 fusion.211
  31.4 0.2 multiply_bitcast_fusion.1
  31.7 0.1 copy.4
  31.8 0.7 gather_fusion
  32.5 0.8 select_select_fusion
  33.4 0.0 all-reduce.4.cloned.1.call-update
  33.4 0.0 reduce-scatter.2.cloned.1.call-start
  33.5 284.0 %all-reduce.4.cloned.1.call-done = f32[32,2,640]{2,1,0:T(2,128)} async-done(((f32[32,2,640]{2,1,0:T(2,128)}), f32[32,2,640]{2,1,0:T(2,128)}) %all-reduce.4.cloned.1.call-update) | async-done | bytes 163856 | tf_op jit(solution)/shard_map/psum | solution.py:140
  317.5 1.1 fusion.212
  318.6 0.1 multiply_add_fusion.4
  318.7 1.9 fusion
  320.6 0.2 multiply_add_fusion
  320.9 1.9 fusion.12
  322.7 0.3 multiply_add_fusion.2
  323.0 1.9 fusion.8
  324.9 1.9 fusion.4
  326.8 3.7 add_add_fusion
  330.5 0.0 reduce-scatter.2.cloned.1.call-update
  330.5 82.4 %reduce-scatter.2.cloned.1.call-done = f32[2,32,501]{2,1,0:T(8,128)} async-done(((f32[32,32,501]{2,1,0:T(8,128)}), f32[2,32,501]{2,1,0:T(8,128)}) %reduce-scatter.2.cloned.1.call-update) | async-done | bytes 128272 | tf_op jit(solution)/shard_map/reduce_scatter | solution.py:158
  (29 shorter events, 0.2 us)
Async XLA Ops:
  6.5 311.0 %all-reduce.4.cloned.1.call-start = ((), (), s32[]{:S(2)}) async-start(), calls=%async_computation.1 | async-start | bytes 327680 | tf_op jit(solution)/shard_map/psum | solution.py:140
  7.3 18.4 %collective-permute-start = (f32[32,60]{1,0:T(8,128)S(1)}, f32[32,60]{1,0:T(8,128)S(1)}, u32[]{:S(2)}, u32[]{:S(2)}) collective-permute-start(f32[32,60]{1,0:T(8,128)S(1)} %slice.131), channel_id=1, source_target_pairs={{0,1},{1,2},{2,3},{3,4},{4,5},{5,6},{6,7},{7,8},{8,9},{9,10},{10,1... | collective-permute-start | bytes 23048 | tf_op jit(solution)/shard_map/ppermute | solution.py:22
  16.9 8.9 %copy-start = (f32[32,2500]{1,0:T(8,128)S(1)}, f32[32,2500]{1,0:T(8,128)}, u32[]{:S(2)}) copy-start(f32[32,2500]{1,0:T(8,128)} %param.2) | copy-start | bytes 960004
  33.4 379.5 %reduce-scatter.2.cloned.1.call-start = ((), (), s32[]{:S(2)}) async-start(), calls=%async_computation.2 | async-start | bytes 2228224 | tf_op jit(solution)/shard_map/reduce_scatter | solution.py:158
Sparse Core Ops, SparseCore 0:
  33.5 283.9 all-reduce.3
  330.6 82.2 reduce-scatter.1
where the time goes:
time: 421 us; the launch traced here: 420 us
  waiting for transfers between devices  367 us (87%)
  matrix products  16 us (4%)
  other arithmetic  15.7 us (4%)
  between operations  13.8 us (3%)
  starting transfers between devices  4.63 us (1%)
    psum x1, waiting for transfers between devices, collect_sources(): return lax.psum(picked, 'chan')  284 us
    reduce_scatter x1, waiting for transfers between devices, body(): lax.psum_scatter(correlate(collected, chan_spec, factor), 'seg', scatter_...  82.4 us
    dot_general x5, matrix products, back_block(): jnp.einsum('sck,kl->scl', joined, inverse_table(block_index, factor), pre...  11.2 us
  transfers between devices with their start and end apart: 3, of which 2 were waited for; matrix products, arithmetic and copies ran while one was open for 3% of the time, Pallas kernels for 0%

commit v1 on v0

v1 whole, which is shorter than its diff:
```python
import math

import jax
import jax.numpy as jnp
import ml_dtypes
import numpy as np
from jax import lax
from jax.experimental import pallas as pl
from jax.experimental.pallas import tpu as pltpu
from jax.sharding import PartitionSpec as P

SEG_LEN = 625
TAPS = 63
MAXLAG = 250
SEGS = 16
SOURCES = 32
ROWS = 32
WIDE = 640
RAW = 2500
NZ, NYH, NX = 8, 4, 4

cutoff = 0.1
water_level = 0.5
epsilon = 1e-06

MESH = pl.DeviceIdType.MESH
f32 = jnp.float32
bf16 = jnp.bfloat16


def split_table(table):
    high = table.astype(np.float32).astype(ml_dtypes.bfloat16)
    low = (table - high.astype(np.float64)).astype(np.float32).astype(ml_dtypes.bfloat16)
    return np.stack([high, low])


def band_table():
    position = np.arange(TAPS, dtype=np.float64)
    window = 0.54 - 0.46 * np.cos(2.0 * math.pi * position / (TAPS - 1))
    taps = window * 2.0 * cutoff * np.sinc(2.0 * cutoff * (position - (TAPS - 1) / 2.0))
    taps = taps / taps.sum()
    index = 4 * np.arange(128)[None, :] + 130 - np.arange(WIDE)[:, None]
    valid = (index >= 0) & (index < TAPS)
    return split_table(np.where(valid, taps[np.clip(index, 0, TAPS - 1)], 0.0))


def forward_table():
    samples = np.arange(WIDE)[:, None]
    freqs = np.arange(WIDE)[None, :]
    phase = ((samples * freqs) % (2 * SEG_LEN)) * (math.pi / SEG_LEN)
    valid = (freqs <= SEG_LEN) & (samples < SEG_LEN)
    table = np.concatenate(
        [np.where(valid, np.cos(phase), 0.0), np.where(valid, -np.sin(phase), 0.0)], axis=1
    )
    return split_table(table)


def split(value):
    high = value.astype(bf16)
    return high, (value - high.astype(f32)).astype(bf16)


def dot(a, b):
    return jnp.dot(a, b, preferred_element_type=f32)


def dot_t(a, b):
    return lax.dot_general(a, b, (((1,), (1,)), ((), ())), preferred_element_type=f32)


def whiten(real_part, imag_part):
    power = real_part * real_part + imag_part * imag_part
    near = power + pltpu.roll(power, 1, 1) + pltpu.roll(power, WIDE - 1, 1)
    smooth = (near + pltpu.roll(power, 2, 1) + pltpu.roll(power, WIDE - 2, 1)) / 5.0
    floor_level = (water_level / (SEG_LEN + 1)) * jnp.sum(power, axis=1, keepdims=True)
    inverse_norm = 1.0 / jnp.sqrt(jnp.maximum(smooth, floor_level) + epsilon)
    return real_part * inverse_norm, imag_part * inverse_norm


def kernel(
    strain, channels, band, table, out,
    raw_high, raw_low, traces, pick, first, second, sources,
    trace_high, trace_low, spec, src_rows, src_spec, cross, table_v,
    table_sem, ag_send, ag_recv, p1_send, p1_recv, p2_send, p2_recv, p3_send, p3_recv,
):
    chan = lax.axis_index("chan")
    seg = lax.axis_index("seg")
    z, yh = chan // NYH, chan % NYH
    x, yl, core = seg // 4, (seg // 2) % 2, seg % 2
    half = seg // 2

    def at(chan_index, seg_index):
        return (chan_index, seg_index)

    def seg_of(x_, yl_, core_):
        return (x_ * 2 + yl_) * 2 + core_

    y_peer = at(chan, seg_of(x, 1 - yl, core))
    core_peer = at(chan, seg_of(x, yl, 1 - core))
    self_exchange = lax.rem(2 * half, NZ) == z

    barrier = pltpu.get_barrier_semaphore()

    def greet(device):
        pl.semaphore_signal(barrier, inc=1, device_id=device, device_id_type=MESH)

    greet(y_peer)
    greet(core_peer)
    for d in range(1, NX):
        greet(at(chan, seg_of(lax.rem(x + d, NX), yl, core)))
    for d in range(1, NYH):
        greet(at(z * NYH + lax.rem(yh + d, NYH), seg))
    for d in range(1, NZ):
        greet(at(lax.rem(z + d, NZ) * NYH + yh, seg))
    q = lax.rem(z - half + NZ, NZ)

    def greet_first(i, carry):
        zs, gs = i // 2, 2 * q + i % 2

        @pl.when(jnp.logical_not((zs == z) & (gs == seg)))
        def _():
            greet(at(zs * NYH + yh, gs))

        return carry

    lax.fori_loop(0, 16, greet_first, 0)

    table_copy = pltpu.make_async_copy(table, table_v, table_sem)
    table_copy.start()

    for ref, part in ((raw_high, 0), (raw_low, 1)):
        ref[:, 0:128] = jnp.zeros((ROWS, 128), bf16)
        ref[:, 2560:2688] = jnp.zeros((ROWS, 128), bf16)
    body = split(strain[:, 0:2432])
    tail = split(strain[:, 2432:RAW])
    raw_high[:, 128:2560] = body[0]
    raw_low[:, 128:2560] = body[1]
    raw_high[:, 2560 : 2560 + 68] = tail[0]
    raw_low[:, 2560 : 2560 + 68] = tail[1]
    win_high = jnp.concatenate([raw_high[:, 512 * b : 512 * b + WIDE] for b in range(5)], axis=0)
    win_low = jnp.concatenate([raw_low[:, 512 * b : 512 * b + WIDE] for b in range(5)], axis=0)
    both = dot(jnp.concatenate([win_high, win_low], axis=0), band[0])
    dec = both[0:160] + both[160:320] + dot(win_high, band[1])
    dec = jnp.concatenate([dec[32 * b : 32 * b + 32] for b in range(5)], axis=1)
    traces[seg] = dec

    local = channels[...] - chan * ROWS
    onehot_t = (lax.broadcasted_iota(jnp.int32, (ROWS, SOURCES), 0) == local).astype(f32)
    picked = lax.dot_general(
        onehot_t, dec, (((0,), (0,)), ((), ())),
        precision=lax.Precision.HIGHEST, preferred_element_type=f32,
    )
    for j in range(SEGS):
        pick[j] = picked[2 * j : 2 * j + 2]

    @pl.when(self_exchange)
    def _():
        pl.semaphore_wait(barrier, 2 + 3 + 3 + 7 + 15)

    @pl.when(jnp.logical_not(self_exchange))
    def _():
        pl.semaphore_wait(barrier, 2 + 3 + 3 + 7 + 16)

    def first_copy(j):
        zd = lax.rem(half + j // 2, NZ)
        slot = z * 2 + core
        return pltpu.make_async_remote_copy(
            src_ref=pick.at[j], dst_ref=first.at[slot],
            send_sem=p1_send.at[j], recv_sem=p1_recv.at[slot],
            device_id=at(zd * NYH + yh, j), device_id_type=MESH,
        )

    def is_self(j):
        return self_exchange & (j == seg)

    def send_first(i, carry):
        j = lax.rem(seg + i, SEGS)

        @pl.when(jnp.logical_not(is_self(j)))
        def _():
            first_copy(j).start()

        return carry

    lax.fori_loop(0, SEGS, send_first, 0)

    @pl.when(self_exchange)
    def _():
        first[z * 2 + core] = pick[seg]

    def ag_copy(slot, index, device):
        return pltpu.make_async_remote_copy(
            src_ref=traces.at[slot], dst_ref=traces.at[slot],
            send_sem=ag_send.at[index], recv_sem=ag_recv.at[slot],
            device_id=device, device_id_type=MESH,
        )

    started = []

    def ag_start(slot, index, device):
        copy = ag_copy(slot, index, device)
        copy.start()
        started.append(copy)

    ag_start(seg, 3, y_peer)
    for d in (1, 3, 2):
        ag_start(seg, d - 1, at(chan, seg_of(lax.rem(x + d, NX), yl, core)))
    ag_start(seg, 7, core_peer)

    def ag_wait(slot):
        ag_copy(slot, 0, core_peer).wait_recv()

    def from_y(d):
        slot = seg_of(lax.rem(x + d, NX), 1 - yl, core)
        ag_wait(slot)
        ag_start(slot, 11 + d, core_peer)

    for d in (3, 1, 2):
        slot = seg_of(lax.rem(x + d, NX), yl, core)
        ag_wait(slot)
        ag_start(slot, 3 + d, y_peer)
        ag_start(slot, 7 + d, core_peer)

    def wait_first(i, carry):
        zs, gs = i // 2, 2 * q + i % 2

        @pl.when(jnp.logical_not((zs == z) & (gs == seg)))
        def _():
            pltpu.make_async_remote_copy(
                src_ref=pick.at[0], dst_ref=first.at[i],
                send_sem=p1_send.at[0], recv_sem=p1_recv.at[i],
                device_id=core_peer, device_id_type=MESH,
            ).wait_recv()

        return carry

    lax.fori_loop(0, 16, wait_first, 0)
    for low in range(2):
        total = first[low]
        for zs in range(1, NZ):
            total = total + first[2 * zs + low]
        second[yh, low] = total

    def second_copy(d):
        return pltpu.make_async_remote_copy(
            src_ref=second.at[yh], dst_ref=second.at[yh],
            send_sem=p2_send.at[d], recv_sem=p2_recv.at[yh],
            device_id=at(z * NYH + lax.rem(yh + d, NYH), seg), device_id_type=MESH,
        )

    for d in (2, 1, 3):
        copy = second_copy(d)
        copy.start()
        started.append(copy)

    for d in (0, 3, 1, 2):
        from_y(d)

    for d in range(1, NYH):
        slot = lax.rem(yh + d, NYH)
        pltpu.make_async_remote_copy(
            src_ref=second.at[slot], dst_ref=second.at[slot],
            send_sem=p2_send.at[d], recv_sem=p2_recv.at[slot],
            device_id=core_peer, device_id_type=MESH,
        ).wait_recv()
    for low in range(2):
        sources[q, low] = second[0, low] + second[1, low] + second[2, low] + second[3, low]

    def third_copy(slot, index, device):
        return pltpu.make_async_remote_copy(
            src_ref=sources.at[slot], dst_ref=sources.at[slot],
            send_sem=p3_send.at[index], recv_sem=p3_recv.at[slot],
            device_id=device, device_id_type=MESH,
        )

    for d in (4, 3, 5, 2, 6, 1, 7):
        copy = third_copy(q, d, at(lax.rem(z + d, NZ) * NYH + yh, seg))
        copy.start()
        started.append(copy)

    for x_ in range(NX):
        for yl_ in range(2):
            ag_wait(seg_of(x_, yl_, 1 - core))

    table_copy.wait()

    lane = lax.broadcasted_iota(jnp.int32, (ROWS, 128), 1)

    def prepare(g, carry):
        before = jnp.maximum(g - 1, 0)
        spill = pltpu.roll(traces[before, :, 512:640], 15, 1)
        head = traces[g, :, 0:128] + jnp.where((lane < 15) & (g > 0), spill, 0.0)
        rows = pl.ds(pl.multiple_of(g * ROWS, ROWS), ROWS)
        trace_high[rows, 0:128], trace_low[rows, 0:128] = split(head)
        trace_high[rows, 128:640], trace_low[rows, 128:640] = split(traces[g, :, 128:640])
        return carry

    lax.fori_loop(0, SEGS, prepare, 0)

    def transform(block, carry):
        rows = pl.ds(pl.multiple_of((block // 5) * 256, 256), 256)
        cols = pl.ds(pl.multiple_of((block % 5) * 256, 256), 256)
        high = trace_high[rows, :]
        t_high = table_v[0, :, cols]
        spec[rows, cols] = (
            dot(high, t_high) + dot(trace_low[rows, :], t_high) + dot(high, table_v[1, :, cols])
        )
        return carry

    lax.fori_loop(0, 10, transform, 0)

    def whiten_rows(g, carry):
        rows = pl.ds(pl.multiple_of(g * ROWS, ROWS), ROWS)
        re, im = whiten(spec[rows, 0:640], spec[rows, 640:1280])
        spec[rows, 0:640] = re
        spec[rows, 640:1280] = im
        return carry

    lax.fori_loop(0, SEGS, whiten_rows, 0)

    for d in range(1, NZ):
        slot = lax.rem(q + d, NZ)
        third_copy(slot, 0, core_peer).wait_recv()
    for g in range(SEGS):
        for e in range(2):
            src_rows[e * 16 + g : e * 16 + g + 1, :] = sources[g // 2, g % 2, e : e + 1, :]
    lane16 = lax.broadcasted_iota(jnp.int32, (16, 128), 1)
    row16 = lax.broadcasted_iota(jnp.int32, (16, 128), 0)
    heads = []
    for e in range(2):
        spill = pltpu.roll(pltpu.roll(src_rows[e * 16 : e * 16 + 16, 512:640], 15, 1), 1, 0)
        keep = (lane16 < 15) & (row16 > 0)
        heads.append(src_rows[e * 16 : e * 16 + 16, 0:128] + jnp.where(keep, spill, 0.0))
    whole = jnp.concatenate([jnp.concatenate(heads, axis=0), src_rows[:, 128:640]], axis=1)
    s_high, s_low = split(whole)
    s_both = jnp.concatenate([s_high, s_low], axis=0)

    def transform_src(block, carry):
        cols = pl.ds(pl.multiple_of(block * 256, 256), 256)
        pair = dot(s_both, table_v[0, :, cols])
        src_spec[:, cols] = pair[0:32] + pair[32:64] + dot(s_high, table_v[1, :, cols])
        return carry

    lax.fori_loop(0, 5, transform_src, 0)
    re, im = whiten(src_spec[:, 0:640], src_spec[:, 640:1280])
    src_spec[:, 0:640] = re
    src_spec[:, 640:1280] = im

    factor = 1.0 / math.sqrt(2.0 * SEG_LEN * SEGS)

    def cross_block(block, carry):
        re_cols = pl.ds(pl.multiple_of(block * 128, 128), 128)
        im_cols = pl.ds(pl.multiple_of(640 + block * 128, 128), 128)
        freq = block * 128 + lane
        weight = jnp.where((freq == 0) | (freq == SEG_LEN), factor, 2.0 * factor)
        acc = [[jnp.zeros((ROWS, 128), f32) for _ in range(2)] for _ in range(2)]
        for g in range(SEGS):
            c_re = spec[g * ROWS : g * ROWS + ROWS, re_cols]
            c_im = spec[g * ROWS : g * ROWS + ROWS, im_cols]
            for e in range(2):
                s_re = src_spec[e * 16 + g : e * 16 + g + 1, re_cols]
                s_im = src_spec[e * 16 + g : e * 16 + g + 1, im_cols]
                acc[e][0] = acc[e][0] + (s_re * c_re + s_im * c_im)
                acc[e][1] = acc[e][1] + (s_re * c_im - s_im * c_re)
        for e in range(2):
            cross[e * ROWS : e * ROWS + ROWS, re_cols] = acc[e][0] * weight
            cross[e * ROWS : e * ROWS + ROWS, im_cols] = acc[e][1] * weight
        return carry

    lax.fori_loop(0, 5, cross_block, 0)

    parts = []
    for base in (0, 640):
        c_high, c_low = split(cross[:, base : base + 640])
        pair = dot_t(jnp.concatenate([c_high, c_low], axis=0), table_v[0, 0:256, base : base + 640])
        parts.append(
            pair[0:64] + pair[64:128] + dot_t(c_high, table_v[1, 0:256, base : base + 640])
        )
    even, odd = parts
    lags = jnp.concatenate([even - odd, even + odd], axis=1)
    l_high, l_low = split(lags)
    l_last = (lags - l_high.astype(f32) - l_low.astype(f32)).astype(bf16)
    row = lax.broadcasted_iota(jnp.int32, (512, 512), 0)
    col = lax.broadcasted_iota(jnp.int32, (512, 512), 1)
    negative = (row > 0) & (row < 256) & (col == MAXLAG - row)
    positive = (row >= 256) & (col == MAXLAG - 256 + row)
    place = jnp.where(negative | positive, 1.0, 0.0).astype(bf16)
    moved = dot(jnp.concatenate([l_high, l_low, l_last], axis=0), place)
    placed = moved[0:64] + moved[64:128] + moved[128:192]
    for e in range(2):
        out[e] = placed[e * ROWS : e * ROWS + ROWS, 0 : 2 * MAXLAG + 1]

    for copy in started:
        copy.wait_send()

    def wait_send_first(j, carry):
        @pl.when(jnp.logical_not(is_self(j)))
        def _():
            first_copy(j).wait_send()

        return carry

    lax.fori_loop(0, SEGS, wait_send_first, 0)


def body(strain, source_channels):
    vmem = pl.BlockSpec(memory_space=pltpu.VMEM)
    sem = pltpu.SemaphoreType.DMA
    return pl.pallas_call(
        kernel,
        out_shape=jax.ShapeDtypeStruct((2, ROWS, 2 * MAXLAG + 1), f32),
        in_specs=[vmem, vmem, vmem, pl.BlockSpec(memory_space=pl.ANY)],
        out_specs=vmem,
        scratch_shapes=[
            pltpu.VMEM((ROWS, 2688), bf16),
            pltpu.VMEM((ROWS, 2688), bf16),
            pltpu.VMEM((SEGS, ROWS, WIDE), f32),
            pltpu.VMEM((SEGS, 2, WIDE), f32),
            pltpu.VMEM((16, 2, WIDE), f32),
            pltpu.VMEM((NYH, 2, 2, WIDE), f32),
            pltpu.VMEM((NZ, 2, 2, WIDE), f32),
            pltpu.VMEM((SEGS * ROWS, WIDE), bf16),
            pltpu.VMEM((SEGS * ROWS, WIDE), bf16),
            pltpu.VMEM((SEGS * ROWS, 2 * WIDE), f32),
            pltpu.VMEM((32, WIDE), f32),
            pltpu.VMEM((32, 2 * WIDE), f32),
            pltpu.VMEM((64, 2 * WIDE), f32),
            pltpu.VMEM((2, WIDE, 2 * WIDE), bf16),
            sem(()), sem((16,)), sem((16,)), sem((16,)), sem((16,)),
            sem((4,)), sem((4,)), sem((8,)), sem((8,)),
        ],
        compiler_params=pltpu.CompilerParams(collective_id=0, has_side_effects=True),
        name="noise_stack",
    )(strain, source_channels.reshape(1, SOURCES), jnp.asarray(band_table()), jnp.asarray(forward_table()))


def solution(mesh):
    in_specs = (P("chan", "seg"), P())
    out_specs = P("seg", "chan", None)
    return jax.shard_map(body, mesh=mesh, in_specs=in_specs, out_specs=out_specs, check_vma=False)
```

time: 421 us -> 47.6 us (0.11)
  the two profiles are of different devices: /device:TPU:1 before, /device:TPU:8 now
where the time goes in v1:
time: 47.6 us; the launch traced here: 47.5 us
  Pallas kernels  45.9 us (96%)
  local copies, waits for them, and re-layouts  1.57 us (3%)
    pallas_call x1, Pallas kernels, body(): pl.pallas_call(kernel, out_shape=jax.ShapeDtypeStruct((2, ROWS, 2 * MAXLA...  45.9 us
    unnamed x1, local copies, waits for them, and re-layouts  1.57 us

profile of v1, /device:TPU:8, one launch (start us, length us, event | category | flops | bytes accessed | tf_op | source)
XLA Modules:
  0.0 47.5 jit_solution(5276848782200978440)
XLA Ops:
  0.0 45.9 %noise_stack.1 = f32[2,32,501]{2,1,0:T(8,128)} custom-call(f32[32,2500]{1,0:T(8,128)} %strain.1, s32[1,32]{1,0:T(1,128)} %bitcast.1, bf16[2,640,128]{2,1,0:T(8,128)(2,1)} %constant.4.clone.band, bf16[2,640,1280]{2,1,0:T(8,128)(2,1)} %constant.5.clone.table), custom_call_target="tpu_custom_call" | custom-call | tf_op jit(solution)/shard_map/noise_stack/pallas_call | solution.py:409
  45.9 1.6 %copy.6 = f32[2,32,501]{2,1,0:T(8,128)} copy(f32[2,32,501]{2,1,0:T(8,128)} %noise_stack.1) | data formatting | bytes 256512

commit v2 on v1

--- a/solution.py
+++ b/solution.py
@@ -71,16 +71,16 @@
 def whiten(real_part, imag_part):
     power = real_part * real_part + imag_part * imag_part
     near = power + pltpu.roll(power, 1, 1) + pltpu.roll(power, WIDE - 1, 1)
-    smooth = (near + pltpu.roll(power, 2, 1) + pltpu.roll(power, WIDE - 2, 1)) / 5.0
+    smooth = (near + pltpu.roll(power, 2, 1) + pltpu.roll(power, WIDE - 2, 1)) * 0.2
     floor_level = (water_level / (SEG_LEN + 1)) * jnp.sum(power, axis=1, keepdims=True)
-    inverse_norm = 1.0 / jnp.sqrt(jnp.maximum(smooth, floor_level) + epsilon)
+    inverse_norm = lax.rsqrt(jnp.maximum(smooth, floor_level) + epsilon)
     return real_part * inverse_norm, imag_part * inverse_norm
 
 
 def kernel(
     strain, channels, band, table, out,
     raw_high, raw_low, traces, pick, first, second, sources,
-    trace_high, trace_low, spec, src_rows, src_spec, cross, table_v,
+    trace_parts, spec, src_rows, src_spec, cross, table_v,
     table_sem, ag_send, ag_recv, p1_send, p1_recv, p2_send, p2_recv, p3_send, p3_recv,
 ):
     chan = lax.axis_index("chan")
@@ -125,8 +125,13 @@
 
     lax.fori_loop(0, 16, greet_first, 0)
 
-    table_copy = pltpu.make_async_copy(table, table_v, table_sem)
-    table_copy.start()
+    table_copies = []
+    for i, part in enumerate((0, 0, 1)):
+        copy = pltpu.make_async_copy(
+            table.at[part], table_v.at[WIDE * i : WIDE * i + WIDE], table_sem.at[i]
+        )
+        copy.start()
+        table_copies.append(copy)
 
     for ref, part in ((raw_high, 0), (raw_low, 1)):
         ref[:, 0:128] = jnp.zeros((ROWS, 128), bf16)
@@ -221,6 +226,42 @@
         ag_start(slot, 3 + d, y_peer)
         ag_start(slot, 7 + d, core_peer)
 
+    for d in (0, 3, 1, 2):
+        from_y(d)
+
+    for x_ in range(NX):
+        for yl_ in range(2):
+            ag_wait(seg_of(x_, yl_, 1 - core))
+
+    for copy in table_copies:
+        copy.wait()
+
+    lane = lax.broadcasted_iota(jnp.int32, (ROWS, 128), 1)
+
+    def prepare(g, carry):
+        before = jnp.maximum(g - 1, 0)
+        spill = pltpu.roll(traces[before, :, 512:640], 15, 1)
+        head = traces[g, :, 0:128] + jnp.where((lane < 15) & (g > 0), spill, 0.0)
+        rows = pl.ds(pl.multiple_of(g * ROWS, ROWS), ROWS)
+        for high, low, first_col, last_col in (
+            (*split(head), 0, 128),
+            (*split(traces[g, :, 128:640]), 128, 640),
+        ):
+            trace_parts[rows, first_col:last_col] = high
+            trace_parts[rows, WIDE + first_col : WIDE + last_col] = low
+            trace_parts[rows, 2 * WIDE + first_col : 2 * WIDE + last_col] = high
+        return carry
+
+    lax.fori_loop(0, SEGS, prepare, 0)
+
+    def transform(block, carry):
+        rows = pl.ds(pl.multiple_of((block // 5) * 256, 256), 256)
+        cols = pl.ds(pl.multiple_of((block % 5) * 256, 256), 256)
+        spec[rows, cols] = dot(trace_parts[rows, :], table_v[:, cols])
+        return carry
+
+    lax.fori_loop(0, 3, transform, 0)
+
     def wait_first(i, carry):
         zs, gs = i // 2, 2 * q + i % 2
 
@@ -253,8 +294,7 @@
         copy.start()
         started.append(copy)
 
-    for d in (0, 3, 1, 2):
-        from_y(d)
+    lax.fori_loop(3, 10, transform, 0)
 
     for d in range(1, NYH):
         slot = lax.rem(yh + d, NYH)
@@ -277,37 +317,6 @@
         copy = third_copy(q, d, at(lax.rem(z + d, NZ) * NYH + yh, seg))
         copy.start()
         started.append(copy)
-
-    for x_ in range(NX):
-        for yl_ in range(2):
-            ag_wait(seg_of(x_, yl_, 1 - core))
-
-    table_copy.wait()
-
-    lane = lax.broadcasted_iota(jnp.int32, (ROWS, 128), 1)
-
-    def prepare(g, carry):
-        before = jnp.maximum(g - 1, 0)
-        spill = pltpu.roll(traces[before, :, 512:640], 15, 1)
-        head = traces[g, :, 0:128] + jnp.where((lane < 15) & (g > 0), spill, 0.0)
-        rows = pl.ds(pl.multiple_of(g * ROWS, ROWS), ROWS)
-        trace_high[rows, 0:128], trace_low[rows, 0:128] = split(head)
-        trace_high[rows, 128:640], trace_low[rows, 128:640] = split(traces[g, :, 128:640])
-        return carry
-
-    lax.fori_loop(0, SEGS, prepare, 0)
-
-    def transform(block, carry):
-        rows = pl.ds(pl.multiple_of((block // 5) * 256, 256), 256)
-        cols = pl.ds(pl.multiple_of((block % 5) * 256, 256), 256)
-        high = trace_high[rows, :]
-        t_high = table_v[0, :, cols]
-        spec[rows, cols] = (
-            dot(high, t_high) + dot(trace_low[rows, :], t_high) + dot(high, table_v[1, :, cols])
-        )
-        return carry
-
-    lax.fori_loop(0, 10, transform, 0)
 
     def whiten_rows(g, carry):
         rows = pl.ds(pl.multiple_of(g * ROWS, ROWS), ROWS)
@@ -337,8 +346,8 @@
 
     def transform_src(block, carry):
         cols = pl.ds(pl.multiple_of(block * 256, 256), 256)
-        pair = dot(s_both, table_v[0, :, cols])
-        src_spec[:, cols] = pair[0:32] + pair[32:64] + dot(s_high, table_v[1, :, cols])
+        pair = dot(s_both, table_v[0:WIDE, cols])
+        src_spec[:, cols] = pair[0:32] + pair[32:64] + dot(s_high, table_v[2 * WIDE : 3 * WIDE, cols])
         return carry
 
     lax.fori_loop(0, 5, transform_src, 0)
@@ -372,9 +381,9 @@
     parts = []
     for base in (0, 640):
         c_high, c_low = split(cross[:, base : base + 640])
-        pair = dot_t(jnp.concatenate([c_high, c_low], axis=0), table_v[0, 0:256, base : base + 640])
+        pair = dot_t(jnp.concatenate([c_high, c_low], axis=0), table_v[0:256, base : base + 640])
         parts.append(
-            pair[0:64] + pair[64:128] + dot_t(c_high, table_v[1, 0:256, base : base + 640])
+            pair[0:64] + pair[64:128] + dot_t(c_high, table_v[2 * WIDE : 2 * WIDE + 256, base : base + 640])
         )
     even, odd = parts
     lags = jnp.concatenate([even - odd, even + odd], axis=1)
@@ -419,14 +428,13 @@
             pltpu.VMEM((16, 2, WIDE), f32),
             pltpu.VMEM((NYH, 2, 2, WIDE), f32),
             pltpu.VMEM((NZ, 2, 2, WIDE), f32),
-            pltpu.VMEM((SEGS * ROWS, WIDE), bf16),
-            pltpu.VMEM((SEGS * ROWS, WIDE), bf16),
+            pltpu.VMEM((SEGS * ROWS, 3 * WIDE), bf16),
             pltpu.VMEM((SEGS * ROWS, 2 * WIDE), f32),
             pltpu.VMEM((32, WIDE), f32),
             pltpu.VMEM((32, 2 * WIDE), f32),
             pltpu.VMEM((64, 2 * WIDE), f32),
-            pltpu.VMEM((2, WIDE, 2 * WIDE), bf16),
-            sem(()), sem((16,)), sem((16,)), sem((16,)), sem((16,)),
+            pltpu.VMEM((3 * WIDE, 2 * WIDE), bf16),
+            sem((3,)), sem((16,)), sem((16,)), sem((16,)), sem((16,)),
             sem((4,)), sem((4,)), sem((8,)), sem((8,)),
         ],
         compiler_params=pltpu.CompilerParams(collective_id=0, has_side_effects=True),

time: 47.6 us -> 48.5 us (1.019)
  the two profiles are of different devices: /device:TPU:8 before, /device:TPU:1 now
where the time goes in v2:
time: 48.5 us; the launch traced here: 48.4 us
  Pallas kernels  46.8 us (96%)
  local copies, waits for them, and re-layouts  1.57 us (3%)
    pallas_call x1, Pallas kernels, body(): pl.pallas_call(kernel, out_shape=jax.ShapeDtypeStruct((2, ROWS, 2 * MAXLA...  46.8 us
    unnamed x1, local copies, waits for them, and re-layouts  1.57 us

profile of v2, /device:TPU:1, one launch (start us, length us, event | category | flops | bytes accessed | tf_op | source)
XLA Modules:
  0.0 48.4 jit_solution(11404804467332818316)
XLA Ops:
  0.0 46.8 %noise_stack.1 = f32[2,32,501]{2,1,0:T(8,128)} custom-call(f32[32,2500]{1,0:T(8,128)} %strain.1, s32[1,32]{1,0:T(1,128)} %bitcast.1, bf16[2,640,128]{2,1,0:T(8,128)(2,1)} %constant.4.clone.band, bf16[2,640,1280]{2,1,0:T(8,128)(2,1)} %constant.5.clone.table), custom_call_target="tpu_custom_call" | custom-call | tf_op jit(solution)/shard_map/noise_stack/pallas_call | solution.py:418
  46.8 1.6 %copy.6 = f32[2,32,501]{2,1,0:T(8,128)} copy(f32[2,32,501]{2,1,0:T(8,128)} %noise_stack.1) | data formatting | bytes 256512

commit v3 on v1

--- a/solution.py
+++ b/solution.py
@@ -71,16 +71,16 @@
 def whiten(real_part, imag_part):
     power = real_part * real_part + imag_part * imag_part
     near = power + pltpu.roll(power, 1, 1) + pltpu.roll(power, WIDE - 1, 1)
-    smooth = (near + pltpu.roll(power, 2, 1) + pltpu.roll(power, WIDE - 2, 1)) / 5.0
+    smooth = (near + pltpu.roll(power, 2, 1) + pltpu.roll(power, WIDE - 2, 1)) * 0.2
     floor_level = (water_level / (SEG_LEN + 1)) * jnp.sum(power, axis=1, keepdims=True)
-    inverse_norm = 1.0 / jnp.sqrt(jnp.maximum(smooth, floor_level) + epsilon)
+    inverse_norm = lax.rsqrt(jnp.maximum(smooth, floor_level) + epsilon)
     return real_part * inverse_norm, imag_part * inverse_norm
 
 
 def kernel(
     strain, channels, band, table, out,
     raw_high, raw_low, traces, pick, first, second, sources,
-    trace_high, trace_low, spec, src_rows, src_spec, cross, table_v,
+    trace_parts, spec, src_rows, src_spec, cross, table_v,
     table_sem, ag_send, ag_recv, p1_send, p1_recv, p2_send, p2_recv, p3_send, p3_recv,
 ):
     chan = lax.axis_index("chan")
@@ -125,8 +125,13 @@
 
     lax.fori_loop(0, 16, greet_first, 0)
 
-    table_copy = pltpu.make_async_copy(table, table_v, table_sem)
-    table_copy.start()
+    table_copies = []
+    for i, part in enumerate((0, 0, 1)):
+        copy = pltpu.make_async_copy(
+            table.at[part], table_v.at[WIDE * i : WIDE * i + WIDE], table_sem.at[i]
+        )
+        copy.start()
+        table_copies.append(copy)
 
     for ref, part in ((raw_high, 0), (raw_low, 1)):
         ref[:, 0:128] = jnp.zeros((ROWS, 128), bf16)
@@ -188,6 +193,12 @@
     def _():
         first[z * 2 + core] = pick[seg]
 
+    started = []
+
+    def begin(copy):
+        copy.start()
+        started.append(copy)
+
     def ag_copy(slot, index, device):
         return pltpu.make_async_remote_copy(
             src_ref=traces.at[slot], dst_ref=traces.at[slot],
@@ -195,31 +206,56 @@
             device_id=device, device_id_type=MESH,
         )
 
-    started = []
-
-    def ag_start(slot, index, device):
-        copy = ag_copy(slot, index, device)
-        copy.start()
-        started.append(copy)
-
-    ag_start(seg, 3, y_peer)
-    for d in (1, 3, 2):
-        ag_start(seg, d - 1, at(chan, seg_of(lax.rem(x + d, NX), yl, core)))
-    ag_start(seg, 7, core_peer)
+    def ag_half(slot, part, index, device):
+        rows = pl.ds(16 * part, 16)
+        recv = ag_recv.at[slot] if part == 0 else ag_recv.at[SEGS]
+        return pltpu.make_async_remote_copy(
+            src_ref=traces.at[slot, rows], dst_ref=traces.at[slot, rows],
+            send_sem=ag_send.at[index], recv_sem=recv,
+            device_id=device, device_id_type=MESH,
+        )
 
     def ag_wait(slot):
         ag_copy(slot, 0, core_peer).wait_recv()
 
-    def from_y(d):
-        slot = seg_of(lax.rem(x + d, NX), 1 - yl, core)
+    def near(d, other):
+        return seg_of(lax.rem(x + d, NX), (1 - yl) if other else yl, core)
+
+    x_next, x_last = at(chan, near(1, 0)), at(chan, near(3, 0))
+
+    def ag_begin():
+        begin(ag_copy(seg, 0, y_peer))
+        begin(ag_copy(seg, 1, x_next))
+        begin(ag_copy(seg, 2, x_last))
+        begin(ag_copy(seg, 3, core_peer))
+
+    def ag_relay_near():
+        slot = near(0, 1)
         ag_wait(slot)
-        ag_start(slot, 11 + d, core_peer)
-
-    for d in (3, 1, 2):
-        slot = seg_of(lax.rem(x + d, NX), yl, core)
+        begin(ag_copy(slot, 4, x_next))
+        begin(ag_copy(slot, 5, x_last))
+        begin(ag_copy(slot, 6, core_peer))
+        slot = near(3, 0)
         ag_wait(slot)
-        ag_start(slot, 3 + d, y_peer)
-        ag_start(slot, 7 + d, core_peer)
+        begin(ag_half(slot, 0, 7, x_next))
+        begin(ag_copy(slot, 8, core_peer))
+        slot = near(1, 0)
+        ag_wait(slot)
+        begin(ag_half(slot, 1, 9, x_last))
+        begin(ag_copy(slot, 10, core_peer))
+
+    def ag_relay_far():
+        slot = near(2, 0)
+        ag_half(slot, 0, 0, core_peer).wait_recv()
+        ag_half(slot, 1, 0, core_peer).wait_recv()
+        begin(ag_copy(slot, 11, y_peer))
+        begin(ag_copy(slot, 12, core_peer))
+        for index, slot in ((13, near(3, 1)), (14, near(1, 1)), (15, near(2, 1))):
+            ag_wait(slot)
+            begin(ag_copy(slot, index, core_peer))
+
+    ag_begin()
+    ag_relay_near()
 
     def wait_first(i, carry):
         zs, gs = i // 2, 2 * q + i % 2
@@ -253,8 +289,7 @@
         copy.start()
         started.append(copy)
 
-    for d in (0, 3, 1, 2):
-        from_y(d)
+    ag_relay_far()
 
     for d in range(1, NYH):
         slot = lax.rem(yh + d, NYH)
@@ -282,7 +317,8 @@
         for yl_ in range(2):
             ag_wait(seg_of(x_, yl_, 1 - core))
 
-    table_copy.wait()
+    for copy in table_copies:
+        copy.wait()
 
     lane = lax.broadcasted_iota(jnp.int32, (ROWS, 128), 1)
 
@@ -291,8 +327,13 @@
         spill = pltpu.roll(traces[before, :, 512:640], 15, 1)
         head = traces[g, :, 0:128] + jnp.where((lane < 15) & (g > 0), spill, 0.0)
         rows = pl.ds(pl.multiple_of(g * ROWS, ROWS), ROWS)
-        trace_high[rows, 0:128], trace_low[rows, 0:128] = split(head)
-        trace_high[rows, 128:640], trace_low[rows, 128:640] = split(traces[g, :, 128:640])
+        for high, low, first_col, last_col in (
+            (*split(head), 0, 128),
+            (*split(traces[g, :, 128:640]), 128, 640),
+        ):
+            trace_parts[rows, first_col:last_col] = high
+            trace_parts[rows, WIDE + first_col : WIDE + last_col] = low
+            trace_parts[rows, 2 * WIDE + first_col : 2 * WIDE + last_col] = high
         return carry
 
     lax.fori_loop(0, SEGS, prepare, 0)
@@ -300,23 +341,19 @@
     def transform(block, carry):
         rows = pl.ds(pl.multiple_of((block // 5) * 256, 256), 256)
         cols = pl.ds(pl.multiple_of((block % 5) * 256, 256), 256)
-        high = trace_high[rows, :]
-        t_high = table_v[0, :, cols]
-        spec[rows, cols] = (
-            dot(high, t_high) + dot(trace_low[rows, :], t_high) + dot(high, table_v[1, :, cols])
-        )
+        spec[rows, cols] = dot(trace_parts[rows, :], table_v[:, cols])
         return carry
 
     lax.fori_loop(0, 10, transform, 0)
 
     def whiten_rows(g, carry):
-        rows = pl.ds(pl.multiple_of(g * ROWS, ROWS), ROWS)
+        rows = pl.ds(pl.multiple_of(g * 128, 128), 128)
         re, im = whiten(spec[rows, 0:640], spec[rows, 640:1280])
         spec[rows, 0:640] = re
         spec[rows, 640:1280] = im
         return carry
 
-    lax.fori_loop(0, SEGS, whiten_rows, 0)
+    lax.fori_loop(0, 4, whiten_rows, 0)
 
     for d in range(1, NZ):
         slot = lax.rem(q + d, NZ)
@@ -337,8 +374,8 @@
 
     def transform_src(block, carry):
         cols = pl.ds(pl.multiple_of(block * 256, 256), 256)
-        pair = dot(s_both, table_v[0, :, cols])
-        src_spec[:, cols] = pair[0:32] + pair[32:64] + dot(s_high, table_v[1, :, cols])
+        pair = dot(s_both, table_v[0:WIDE, cols])
+        src_spec[:, cols] = pair[0:32] + pair[32:64] + dot(s_high, table_v[2 * WIDE : 3 * WIDE, cols])
         return carry
 
     lax.fori_loop(0, 5, transform_src, 0)
@@ -372,9 +409,9 @@
     parts = []
     for base in (0, 640):
         c_high, c_low = split(cross[:, base : base + 640])
-        pair = dot_t(jnp.concatenate([c_high, c_low], axis=0), table_v[0, 0:256, base : base + 640])
+        pair = dot_t(jnp.concatenate([c_high, c_low], axis=0), table_v[0:256, base : base + 640])
         parts.append(
-            pair[0:64] + pair[64:128] + dot_t(c_high, table_v[1, 0:256, base : base + 640])
+            pair[0:64] + pair[64:128] + dot_t(c_high, table_v[2 * WIDE : 2 * WIDE + 256, base : base + 640])
         )
     even, odd = parts
     lags = jnp.concatenate([even - odd, even + odd], axis=1)
@@ -419,14 +456,13 @@
             pltpu.VMEM((16, 2, WIDE), f32),
             pltpu.VMEM((NYH, 2, 2, WIDE), f32),
             pltpu.VMEM((NZ, 2, 2, WIDE), f32),
-            pltpu.VMEM((SEGS * ROWS, WIDE), bf16),
-            pltpu.VMEM((SEGS * ROWS, WIDE), bf16),
+            pltpu.VMEM((SEGS * ROWS, 3 * WIDE), bf16),
             pltpu.VMEM((SEGS * ROWS, 2 * WIDE), f32),
             pltpu.VMEM((32, WIDE), f32),
             pltpu.VMEM((32, 2 * WIDE), f32),
             pltpu.VMEM((64, 2 * WIDE), f32),
-            pltpu.VMEM((2, WIDE, 2 * WIDE), bf16),
-            sem(()), sem((16,)), sem((16,)), sem((16,)), sem((16,)),
+            pltpu.VMEM((3 * WIDE, 2 * WIDE), bf16),
+            sem((3,)), sem((16,)), sem((17,)), sem((16,)), sem((16,)),
             sem((4,)), sem((4,)), sem((8,)), sem((8,)),
         ],
         compiler_params=pltpu.CompilerParams(collective_id=0, has_side_effects=True),

time: 47.6 us -> 42.7 us (0.90)
  the two profiles are of different devices: /device:TPU:8 before, /device:TPU:1 now
where the time goes in v3:
time: 42.7 us; the launch traced here: 42.5 us
  Pallas kernels  41 us (96%)
  local copies, waits for them, and re-layouts  1.57 us (4%)
    pallas_call x1, Pallas kernels, body(): pl.pallas_call(kernel, out_shape=jax.ShapeDtypeStruct((2, ROWS, 2 * MAXLA...  41 us
    unnamed x1, local copies, waits for them, and re-layouts  1.57 us

profile of v3, /device:TPU:1, one launch (start us, length us, event | category | flops | bytes accessed | tf_op | source)
XLA Modules:
  0.0 42.5 jit_solution(6962174712128797914)
XLA Ops:
  0.0 41.0 %noise_stack.1 = f32[2,32,501]{2,1,0:T(8,128)} custom-call(f32[32,2500]{1,0:T(8,128)} %strain.1, s32[1,32]{1,0:T(1,128)} %bitcast.1, bf16[2,640,128]{2,1,0:T(8,128)(2,1)} %constant.4.clone.band, bf16[2,640,1280]{2,1,0:T(8,128)(2,1)} %constant.5.clone.table), custom_call_target="tpu_custom_call" | custom-call | tf_op jit(solution)/shard_map/noise_stack/pallas_call | solution.py:446
  41.0 1.6 %copy.6 = f32[2,32,501]{2,1,0:T(8,128)} copy(f32[2,32,501]{2,1,0:T(8,128)} %noise_stack.1) | data formatting | bytes 256512

commit v4 on v3

--- a/solution.py
+++ b/solution.py
@@ -78,9 +78,9 @@
 
 
 def kernel(
-    strain, channels, band, table, out,
-    raw_high, raw_low, traces, pick, first, second, sources,
-    trace_parts, spec, src_rows, src_spec, cross, table_v,
+    strain_in, channels_in, band_in, table, out,
+    strain, channels, band, place, raw_high, raw_low, traces, pick, first, second, sources,
+    trace_parts, spills, spill_table, spec, src_rows, src_last, src_spec, cross, table_v,
     table_sem, ag_send, ag_recv, p1_send, p1_recv, p2_send, p2_recv, p3_send, p3_recv,
 ):
     chan = lax.axis_index("chan")
@@ -125,6 +125,13 @@
 
     lax.fori_loop(0, 16, greet_first, 0)
 
+    inputs = []
+    for i, (source, target) in enumerate(
+        ((strain_in, strain), (band_in, band), (channels_in, channels))
+    ):
+        copy = pltpu.make_async_copy(source, target, table_sem.at[3 + i])
+        copy.start()
+        inputs.append(copy)
     table_copies = []
     for i, part in enumerate((0, 0, 1)):
         copy = pltpu.make_async_copy(
@@ -136,6 +143,8 @@
     for ref, part in ((raw_high, 0), (raw_low, 1)):
         ref[:, 0:128] = jnp.zeros((ROWS, 128), bf16)
         ref[:, 2560:2688] = jnp.zeros((ROWS, 128), bf16)
+    for copy in inputs:
+        copy.wait()
     body = split(strain[:, 0:2432])
     tail = split(strain[:, 2432:RAW])
     raw_high[:, 128:2560] = body[0]
@@ -254,8 +263,64 @@
             ag_wait(slot)
             begin(ag_copy(slot, index, core_peer))
 
+    lane = lax.broadcasted_iota(jnp.int32, (ROWS, 128), 1)
+
+    def slot_of(place_index):
+        group, i = place_index // 4, place_index % 4
+        far, twin = group // 2, group % 2
+        d_near = jnp.where(i < 2, 0, jnp.where(i == 2, 3, 1))
+        d_far = jnp.where(i < 2, 2, jnp.where(i == 2, 3, 1))
+        other_near = jnp.where(i == 1, 1, 0)
+        other_far = jnp.where(i == 0, 0, 1)
+        d = jnp.where(far == 1, d_far, d_near)
+        other = jnp.where(far == 1, other_far, other_near)
+        return (lax.rem(x + d, NX) * 2 + lax.rem(yl + other, 2)) * 2 + lax.rem(core + twin, 2)
+
+    def rows_of(place_index):
+        return pl.ds(pl.multiple_of(place_index * ROWS, ROWS), ROWS)
+
+    def store_parts(place_index, first_col, last_col, value):
+        rows = rows_of(place_index)
+        high, low = split(value)
+        trace_parts[rows, first_col:last_col] = high
+        trace_parts[rows, WIDE + first_col : WIDE + last_col] = low
+        trace_parts[rows, 2 * WIDE + first_col : 2 * WIDE + last_col] = high
+
+    def prepare_four(group):
+        def prepare(i, carry):
+            store_parts(i, 0, 640, traces[slot_of(i)])
+            return carry
+
+        lax.fori_loop(4 * group, 4 * group + 4, prepare, 0)
+
+    def transform(rows, first_row):
+        def block(i, carry):
+            at_rows = pl.ds(first_row, rows)
+            cols = pl.ds(pl.multiple_of(i * 256, 256), 256)
+            spec[at_rows, cols] = dot(trace_parts[at_rows, :], table_v[:, cols])
+            return carry
+
+        lax.fori_loop(0, 5, block, 0)
+
+    def partner(d, other):
+        return seg_of(lax.rem(x + d, NX), (1 - yl) if other else yl, 1 - core)
+
     ag_begin()
     ag_relay_near()
+    prepare_four(0)
+    for copy in table_copies:
+        copy.wait()
+    spill_table[...] = jnp.zeros((128, 2 * WIDE), bf16)
+    spill_table[0:16, :] = table_v[0:16, :]
+    spill_table[16:32, :] = table_v[0:16, :]
+    spill_table[32:48, :] = table_v[2 * WIDE : 2 * WIDE + 16, :]
+    transform(128, 0)
+
+    row = lax.broadcasted_iota(jnp.int32, (512, 512), 0)
+    col = lax.broadcasted_iota(jnp.int32, (512, 512), 1)
+    negative = (row > 0) & (row < 256) & (col == MAXLAG - row)
+    positive = (row >= 256) & (col == MAXLAG - 256 + row)
+    place[...] = jnp.where(negative | positive, 1.0, 0.0).astype(bf16)
 
     def wait_first(i, carry):
         zs, gs = i // 2, 2 * q + i % 2
@@ -289,7 +354,12 @@
         copy.start()
         started.append(copy)
 
+    for d, other in ((0, 0), (0, 1), (3, 0), (1, 0)):
+        ag_wait(partner(d, other))
+    prepare_four(1)
+    transform(128, 128)
     ag_relay_far()
+    prepare_four(2)
 
     for d in range(1, NYH):
         slot = lax.rem(yh + d, NYH)
@@ -313,42 +383,30 @@
         copy.start()
         started.append(copy)
 
-    for x_ in range(NX):
-        for yl_ in range(2):
-            ag_wait(seg_of(x_, yl_, 1 - core))
-
-    for copy in table_copies:
-        copy.wait()
-
-    lane = lax.broadcasted_iota(jnp.int32, (ROWS, 128), 1)
-
-    def prepare(g, carry):
-        before = jnp.maximum(g - 1, 0)
-        spill = pltpu.roll(traces[before, :, 512:640], 15, 1)
-        head = traces[g, :, 0:128] + jnp.where((lane < 15) & (g > 0), spill, 0.0)
-        rows = pl.ds(pl.multiple_of(g * ROWS, ROWS), ROWS)
-        for high, low, first_col, last_col in (
-            (*split(head), 0, 128),
-            (*split(traces[g, :, 128:640]), 128, 640),
-        ):
-            trace_parts[rows, first_col:last_col] = high
-            trace_parts[rows, WIDE + first_col : WIDE + last_col] = low
-            trace_parts[rows, 2 * WIDE + first_col : 2 * WIDE + last_col] = high
-        return carry
-
-    lax.fori_loop(0, SEGS, prepare, 0)
-
-    def transform(block, carry):
-        rows = pl.ds(pl.multiple_of((block // 5) * 256, 256), 256)
-        cols = pl.ds(pl.multiple_of((block % 5) * 256, 256), 256)
-        spec[rows, cols] = dot(trace_parts[rows, :], table_v[:, cols])
-        return carry
-
-    lax.fori_loop(0, 10, transform, 0)
+    for d, other in ((2, 0), (2, 1), (3, 1), (1, 1)):
+        ag_wait(partner(d, other))
+    prepare_four(3)
+
+    def place_spill(i, carry):
+        g = slot_of(i)
+        last = traces[jnp.maximum(g - 1, 0), :, 512:640]
+        high, low = split(jnp.where(g > 0, last, 0.0))
+        high, low = high.astype(f32), low.astype(f32)
+        parts = jnp.where(lane < 15, pltpu.roll(high, 15, 1), 0.0)
+        parts = jnp.where((lane >= 16) & (lane < 31), pltpu.roll(low, 31, 1), parts)
+        parts = jnp.where((lane >= 32) & (lane < 47), pltpu.roll(high, 47, 1), parts)
+        spills[rows_of(i), :] = parts.astype(bf16)
+        return carry
+
+    lax.fori_loop(0, SEGS, place_spill, 0)
+    transform(256, 256)
 
     def whiten_rows(g, carry):
         rows = pl.ds(pl.multiple_of(g * 128, 128), 128)
-        re, im = whiten(spec[rows, 0:640], spec[rows, 640:1280])
+        early = dot(spills[rows, :], spill_table[...])
+        re, im = whiten(
+            spec[rows, 0:640] + early[:, 0:640], spec[rows, 640:1280] + early[:, 640:1280]
+        )
         spec[rows, 0:640] = re
         spec[rows, 640:1280] = im
         return carry
@@ -358,17 +416,16 @@
     for d in range(1, NZ):
         slot = lax.rem(q + d, NZ)
         third_copy(slot, 0, core_peer).wait_recv()
-    for g in range(SEGS):
+    for p in range(SEGS):
+        g = slot_of(p)
+        prev = jnp.maximum(g - 1, 0)
         for e in range(2):
-            src_rows[e * 16 + g : e * 16 + g + 1, :] = sources[g // 2, g % 2, e : e + 1, :]
-    lane16 = lax.broadcasted_iota(jnp.int32, (16, 128), 1)
-    row16 = lax.broadcasted_iota(jnp.int32, (16, 128), 0)
-    heads = []
-    for e in range(2):
-        spill = pltpu.roll(pltpu.roll(src_rows[e * 16 : e * 16 + 16, 512:640], 15, 1), 1, 0)
-        keep = (lane16 < 15) & (row16 > 0)
-        heads.append(src_rows[e * 16 : e * 16 + 16, 0:128] + jnp.where(keep, spill, 0.0))
-    whole = jnp.concatenate([jnp.concatenate(heads, axis=0), src_rows[:, 128:640]], axis=1)
+            row = e * 16 + p
+            src_rows[row : row + 1, :] = sources[g // 2, g % 2, e : e + 1, :]
+            last = sources[prev // 2, prev % 2, e : e + 1, 512:640]
+            src_last[row : row + 1, :] = jnp.where(g > 0, last, 0.0)
+    spill = jnp.where(lane < 15, pltpu.roll(src_last[...], 15, 1), 0.0)
+    whole = jnp.concatenate([src_rows[:, 0:128] + spill, src_rows[:, 128:640]], axis=1)
     s_high, s_low = split(whole)
     s_both = jnp.concatenate([s_high, s_low], axis=0)
 
@@ -417,12 +474,7 @@
     lags = jnp.concatenate([even - odd, even + odd], axis=1)
     l_high, l_low = split(lags)
     l_last = (lags - l_high.astype(f32) - l_low.astype(f32)).astype(bf16)
-    row = lax.broadcasted_iota(jnp.int32, (512, 512), 0)
-    col = lax.broadcasted_iota(jnp.int32, (512, 512), 1)
-    negative = (row > 0) & (row < 256) & (col == MAXLAG - row)
-    positive = (row >= 256) & (col == MAXLAG - 256 + row)
-    place = jnp.where(negative | positive, 1.0, 0.0).astype(bf16)
-    moved = dot(jnp.concatenate([l_high, l_low, l_last], axis=0), place)
+    moved = dot(jnp.concatenate([l_high, l_low, l_last], axis=0), place[...])
     placed = moved[0:64] + moved[64:128] + moved[128:192]
     for e in range(2):
         out[e] = placed[e * ROWS : e * ROWS + ROWS, 0 : 2 * MAXLAG + 1]
@@ -446,9 +498,13 @@
     return pl.pallas_call(
         kernel,
         out_shape=jax.ShapeDtypeStruct((2, ROWS, 2 * MAXLAG + 1), f32),
-        in_specs=[vmem, vmem, vmem, pl.BlockSpec(memory_space=pl.ANY)],
+        in_specs=[pl.BlockSpec(memory_space=pl.ANY)] * 4,
         out_specs=vmem,
         scratch_shapes=[
+            pltpu.VMEM((ROWS, RAW), f32),
+            pltpu.VMEM((1, SOURCES), jnp.int32),
+            pltpu.VMEM((2, WIDE, 128), bf16),
+            pltpu.VMEM((512, 512), bf16),
             pltpu.VMEM((ROWS, 2688), bf16),
             pltpu.VMEM((ROWS, 2688), bf16),
             pltpu.VMEM((SEGS, ROWS, WIDE), f32),
@@ -457,12 +513,15 @@
             pltpu.VMEM((NYH, 2, 2, WIDE), f32),
             pltpu.VMEM((NZ, 2, 2, WIDE), f32),
             pltpu.VMEM((SEGS * ROWS, 3 * WIDE), bf16),
+            pltpu.VMEM((SEGS * ROWS, 128), bf16),
+            pltpu.VMEM((128, 2 * WIDE), bf16),
             pltpu.VMEM((SEGS * ROWS, 2 * WIDE), f32),
             pltpu.VMEM((32, WIDE), f32),
+            pltpu.VMEM((32, 128), f32),
             pltpu.VMEM((32, 2 * WIDE), f32),
             pltpu.VMEM((64, 2 * WIDE), f32),
             pltpu.VMEM((3 * WIDE, 2 * WIDE), bf16),
-            sem((3,)), sem((16,)), sem((17,)), sem((16,)), sem((16,)),
+            sem((6,)), sem((16,)), sem((17,)), sem((16,)), sem((16,)),
             sem((4,)), sem((4,)), sem((8,)), sem((8,)),
         ],
         compiler_params=pltpu.CompilerParams(collective_id=0, has_side_effects=True),

time: 42.7 us -> 40.6 us (0.951)
  Pallas kernels: 41 us -> 38.9 us
    pallas_call x1, Pallas kernels: 41 us -> 38.9 us  [body(): pl.pallas_call(kernel, out_shape=jax.ShapeDtypeStruct((2, ROWS, 2 * MAXLA...]
where the time goes in v4:
time: 40.6 us; the launch traced here: 40.5 us
  Pallas kernels  38.9 us (96%)
  local copies, waits for them, and re-layouts  1.57 us (4%)
    pallas_call x1, Pallas kernels, body(): pl.pallas_call(kernel, out_shape=jax.ShapeDtypeStruct((2, ROWS, 2 * MAXLA...  38.9 us
    unnamed x1, local copies, waits for them, and re-layouts  1.57 us

profile of v4, /device:TPU:1, one launch (start us, length us, event | category | flops | bytes accessed | tf_op | source)
XLA Modules:
  0.0 40.5 jit_solution(5518082327246660721)
XLA Ops:
  0.0 38.9 %noise_stack.1 = f32[2,32,501]{2,1,0:T(8,128)} custom-call(f32[32,2500]{1,0:T(8,128)} %strain_in.1, s32[1,32]{1,0:T(1,128)} %bitcast.1, bf16[2,640,128]{2,1,0:T(8,128)(2,1)} %constant.4.clone.band_in, bf16[2,640,1280]{2,1,0:T(8,128)(2,1)} %constant.5.clone.table), custom_call_target="tpu_custom_call" | custom-call | tf_op jit(solution)/shard_map/noise_stack/pallas_call | solution.py:498
  38.9 1.6 %copy.6 = f32[2,32,501]{2,1,0:T(8,128)} copy(f32[2,32,501]{2,1,0:T(8,128)} %noise_stack.1) | data formatting | bytes 256512

commit v5 on v4

--- a/solution.py
+++ b/solution.py
@@ -99,6 +99,14 @@
     core_peer = at(chan, seg_of(x, yl, 1 - core))
     self_exchange = lax.rem(2 * half, NZ) == z
 
+    inputs = []
+    for i, (source, target) in enumerate(
+        ((strain_in, strain), (band_in, band), (channels_in, channels))
+    ):
+        copy = pltpu.make_async_copy(source, target, table_sem.at[3 + i])
+        copy.start()
+        inputs.append(copy)
+
     barrier = pltpu.get_barrier_semaphore()
 
     def greet(device):
@@ -125,13 +133,6 @@
 
     lax.fori_loop(0, 16, greet_first, 0)
 
-    inputs = []
-    for i, (source, target) in enumerate(
-        ((strain_in, strain), (band_in, band), (channels_in, channels))
-    ):
-        copy = pltpu.make_async_copy(source, target, table_sem.at[3 + i])
-        copy.start()
-        inputs.append(copy)
     table_copies = []
     for i, part in enumerate((0, 0, 1)):
         copy = pltpu.make_async_copy(
@@ -360,6 +361,7 @@
     transform(128, 128)
     ag_relay_far()
     prepare_four(2)
+    transform(128, 256)
 
     for d in range(1, NYH):
         slot = lax.rem(yh + d, NYH)
@@ -399,7 +401,7 @@
         return carry
 
     lax.fori_loop(0, SEGS, place_spill, 0)
-    transform(256, 256)
+    transform(128, 384)
 
     def whiten_rows(g, carry):
         rows = pl.ds(pl.multiple_of(g * 128, 128), 128)
@@ -435,7 +437,7 @@
         src_spec[:, cols] = pair[0:32] + pair[32:64] + dot(s_high, table_v[2 * WIDE : 3 * WIDE, cols])
         return carry
 
-    lax.fori_loop(0, 5, transform_src, 0)
+    lax.fori_loop(0, 5, transform_src, 0, unroll=True)
     re, im = whiten(src_spec[:, 0:640], src_spec[:, 640:1280])
     src_spec[:, 0:640] = re
     src_spec[:, 640:1280] = im

time: 40.6 us -> 39.7 us (0.978)
  Pallas kernels: 38.9 us -> 38 us
    pallas_call x1, Pallas kernels: 38.9 us -> 38 us  [body(): pl.pallas_call(kernel, out_shape=jax.ShapeDtypeStruct((2, ROWS, 2 * MAXLA...]
where the time goes in v5:
time: 39.7 us; the launch traced here: 39.6 us
  Pallas kernels  38 us (96%)
  local copies, waits for them, and re-layouts  1.57 us (4%)
    pallas_call x1, Pallas kernels, body(): pl.pallas_call(kernel, out_shape=jax.ShapeDtypeStruct((2, ROWS, 2 * MAXLA...  38 us
    unnamed x1, local copies, waits for them, and re-layouts  1.57 us

profile of v5, /device:TPU:1, one launch (start us, length us, event | category | flops | bytes accessed | tf_op | source)
XLA Modules:
  0.0 39.6 jit_solution(16967538487690844161)
XLA Ops:
  0.0 38.0 %noise_stack.1 = f32[2,32,501]{2,1,0:T(8,128)} custom-call(f32[32,2500]{1,0:T(8,128)} %strain_in.1, s32[1,32]{1,0:T(1,128)} %bitcast.1, bf16[2,640,128]{2,1,0:T(8,128)(2,1)} %constant.4.clone.band_in, bf16[2,640,1280]{2,1,0:T(8,128)(2,1)} %constant.5.clone.table), custom_call_target="tpu_custom_call" | custom-call | tf_op jit(solution)/shard_map/noise_stack/pallas_call | solution.py:500
  38.0 1.6 %copy.6 = f32[2,32,501]{2,1,0:T(8,128)} copy(f32[2,32,501]{2,1,0:T(8,128)} %noise_stack.1) | data formatting | bytes 256512
